TPU v7x, 32 devices: a whole 2x2x4 slice. The times are simulated.
32 devices in a mesh: dp: 16 (over z, x, core), tensor: 2 (over y).
Axes of the slice: x: 2, y: 2, z: 4, core: 2. Of those that a mesh axis runs over, the one named last changes fastest.
Arguments:
- inputs: bfloat16 [2048, 2048], P('dp'), may hold values from -6 to 6
- segments: int32 [2048], P('dp'), may hold values from 0 to 1, as said below
- positions: int32 [2048], P('dp'), may hold values from 0 to 1999, as said below
- w_query: bfloat16 [2048, 2048], P('dp', 'tensor')
- w_key: bfloat16 [2048, 512], P('dp', 'tensor')
- w_value: bfloat16 [2048, 512], P('dp', 'tensor'), may hold values from -0.125 to 0.125
- w_out: bfloat16 [2048, 2048], P('dp', 'tensor'), may hold values from -0.5 to 0.5
- w_gate: bfloat16 [2048, 8192], P('dp', 'tensor'), may hold values from -0.125 to 0.125
- w_up: bfloat16 [2048, 8192], P('dp', 'tensor'), may hold values from -0.125 to 0.125
- w_down: bfloat16 [2048, 8192], P('dp', 'tensor'), may hold values from -0.125 to 0.125
- attn_gain: bfloat16 [2048], P('dp'), may hold values from 0.5 to 1.5
- mlp_gain: bfloat16 [2048], P('dp'), may hold values from 0.5 to 1.5
- out_grad: bfloat16 [2048, 2048], P('dp'), may hold values from -6 to 6
Outputs:
- output: bfloat16 [2048, 2048], P('dp')
- input_grad: float32 [2048, 2048], P('dp')
- query_grad: float32 [2048, 2048], P('dp', 'tensor')
- key_grad: float32 [2048, 512], P('dp', 'tensor')
- value_grad: float32 [2048, 512], P('dp', 'tensor')
- out_proj_grad: float32 [2048, 2048], P('dp', 'tensor')
- gate_grad: float32 [2048, 8192], P('dp', 'tensor')
- up_grad: float32 [2048, 8192], P('dp', 'tensor')
- down_grad: float32 [2048, 8192], P('dp', 'tensor')
- attn_gain_grad: float32 [2048], P('dp')
- mlp_gain_grad: float32 [2048], P('dp')
Inputs may be any that keep to these rules, and one draw needn't show every extreme that they name: `segments`: within each sequence of 128 tokens segment numbers start at 0 and rise by one where a document begins; documents span 200 to 2000 tokens of the packed stream, so a sequence's first document may have begun in the sequence before it. `positions`: A token's position within its document: it rises by one from token to token of a document and is 0 where a document begins; at a sequence's first token it continues a document that began earlier.
All inputs are finite; a program needn't handle non-finite values.
Results may differ from a plain program's by a relative error of at most 0.019.
The roundings to bfloat16 on the way count: a program that leaves them out, or rounds other values in their place, can miss the bound.
Values may be sent and summed in bfloat16 or wider, within the bound.
No kernel may reach another device: no remote copies, remote signals or barrier semaphores. Data moves between devices by JAX's collectives and lax.ppermute only.
A program may use at most 256 MiB of HBM per device.

v0:
```python
import math
import jax
import jax.numpy as jnp
from jax import lax
from jax.sharding import PartitionSpec as P

HEADS = 32
KV_HEADS = 8
HEAD_DIM = 64
norm_eps = 1e-05
rope_base = 500000.0
masked_score = -1e30


def rope_freqs(head_dim):
    index = jnp.arange(head_dim // 2, dtype=jnp.float32)
    inverse = rope_base ** (-2.0 * index / head_dim)
    wavelen = 2.0 * math.pi / inverse
    smooth = (8192.0 / wavelen - 1.0) / 3.0
    scaled = (1.0 - smooth) * inverse / 32.0 + smooth * inverse
    return jnp.where(wavelen < 2048.0, inverse, jnp.where(wavelen > 8192.0, inverse / 32.0, scaled))


def rotate(values, cosine, sine):
    half = values.shape[-1] // 2
    first = values[..., :half]
    second = values[..., half:]
    return jnp.concatenate(
        [first * cosine - second * sine, second * cosine + first * sine], axis=-1
    )


def norm_parts(values):
    scale = lax.rsqrt(jnp.mean(values * values, axis=-1, keepdims=True) + norm_eps)
    return (values * scale, scale)


def norm_back(grad, unit, scale, gain):
    weighted = grad * gain
    return (
        scale * (weighted - unit * jnp.mean(weighted * unit, axis=-1, keepdims=True)),
        jnp.sum(grad * unit, axis=0),
    )


def dot_last(left, right):
    return lax.dot_general(
        left, right, (((1,), (1,)), ((), ())), preferred_element_type=jnp.float32
    )


def dot_first(left, right):
    return lax.dot_general(
        left, right, (((0,), (0,)), ((), ())), preferred_element_type=jnp.float32
    )


def on_device(
    inputs,
    segments,
    positions,
    w_query,
    w_key,
    w_value,
    w_out,
    w_gate,
    w_up,
    w_down,
    attn_gain,
    mlp_gain,
    out_grad,
):
    length = inputs.shape[0]
    group = HEADS // KV_HEADS
    factor = HEAD_DIM ** (-0.5)
    residual = inputs.astype(jnp.float32)
    angle = positions.astype(jnp.float32)[:, None] * rope_freqs(HEAD_DIM)[None, :]
    cosine = jnp.cos(angle)[:, None, :]
    sine = jnp.sin(angle)[:, None, :]
    order = jnp.arange(length)
    allowed = (segments[:, None] == segments[None, :]) & (order[:, None] >= order[None, :])
    query_full, key_full, value_full, out_full, gain_one = (
        lax.all_gather(w_query, "dp", axis=0, tiled=True),
        lax.all_gather(w_key, "dp", axis=0, tiled=True),
        lax.all_gather(w_value, "dp", axis=0, tiled=True),
        lax.all_gather(w_out, "dp", axis=0, tiled=True),
        lax.all_gather(attn_gain, "dp", axis=0, tiled=True),
    )
    gain_one = gain_one.astype(jnp.float32)
    unit_one, scale_one = norm_parts(residual)
    normed_one = (unit_one * gain_one).astype(jnp.bfloat16)
    query_rot = rotate(
        jnp.dot(normed_one, query_full, preferred_element_type=jnp.float32).reshape(
            length, -1, HEAD_DIM
        ),
        cosine,
        sine,
    ).astype(jnp.bfloat16)
    key_rot = rotate(
        jnp.dot(normed_one, key_full, preferred_element_type=jnp.float32).reshape(
            length, -1, HEAD_DIM
        ),
        cosine,
        sine,
    ).astype(jnp.bfloat16)
    value_heads = (
        jnp.dot(normed_one, value_full, preferred_element_type=jnp.float32)
        .astype(jnp.bfloat16)
        .reshape(length, -1, HEAD_DIM)
    )
    kv_local = key_rot.shape[1]
    query_group = query_rot.reshape(length, kv_local, group, HEAD_DIM)
    scores = jnp.where(
        allowed,
        jnp.einsum("qhgd,khd->hgqk", query_group, key_rot, preferred_element_type=jnp.float32)
        * factor,
        masked_score,
    )
    top = jnp.max(scores, axis=-1, keepdims=True)
    expo = jnp.exp(scores - top)
    total = jnp.sum(expo, axis=-1, keepdims=True)
    log_total = top + jnp.log(total)
    weights_low = (expo / total).astype(jnp.bfloat16)
    attended = (
        jnp.einsum("hgqk,khd->qhgd", weights_low, value_heads, preferred_element_type=jnp.float32)
        .astype(jnp.bfloat16)
        .reshape(length, -1)
    )
    attn_out = lax.psum(dot_last(attended, out_full), "tensor")
    middle = residual + attn_out
    gate_full, up_full, down_full, gain_two = (
        lax.all_gather(w_gate, "dp", axis=0, tiled=True),
        lax.all_gather(w_up, "dp", axis=0, tiled=True),
        lax.all_gather(w_down, "dp", axis=0, tiled=True),
        lax.all_gather(mlp_gain, "dp", axis=0, tiled=True),
    )
    gain_two = gain_two.astype(jnp.float32)
    unit_two, scale_two = norm_parts(middle)
    normed_two = (unit_two * gain_two).astype(jnp.bfloat16)
    gate = jnp.dot(normed_two, gate_full, preferred_element_type=jnp.float32)
    upward = jnp.dot(normed_two, up_full, preferred_element_type=jnp.float32)
    sigma = jax.nn.sigmoid(gate)
    active = (gate * sigma * upward).astype(jnp.bfloat16)
    mlp_out = lax.psum(dot_last(active, down_full).astype(jnp.bfloat16), "tensor").astype(
        jnp.float32
    )
    output = (middle + mlp_out).astype(jnp.bfloat16)
    gate_back, up_back, down_back, gain_back = (
        lax.all_gather(w_gate, "dp", axis=0, tiled=True),
        lax.all_gather(w_up, "dp", axis=0, tiled=True),
        lax.all_gather(w_down, "dp", axis=0, tiled=True),
        lax.all_gather(mlp_gain, "dp", axis=0, tiled=True),
    )
    gain_back = gain_back.astype(jnp.float32)
    down_grad = dot_first(out_grad, active)
    active_grad = jnp.dot(out_grad, down_back, preferred_element_type=jnp.float32)
    gate_delta = (active_grad * upward * sigma * (1.0 + gate * (1.0 - sigma))).astype(jnp.bfloat16)
    up_delta = (active_grad * gate * sigma).astype(jnp.bfloat16)
    gate_grad = dot_first(normed_two, gate_delta)
    up_grad = dot_first(normed_two, up_delta)
    normed_two_grad = lax.psum(
        dot_last(gate_delta, gate_back) + dot_last(up_delta, up_back), "tensor"
    )
    middle_part, mlp_gain_grad = norm_back(normed_two_grad, unit_two, scale_two, gain_back)
    middle_grad = out_grad.astype(jnp.float32) + middle_part
    query_back, key_back, value_back, out_back, gain_first = (
        lax.all_gather(w_query, "dp", axis=0, tiled=True),
        lax.all_gather(w_key, "dp", axis=0, tiled=True),
        lax.all_gather(w_value, "dp", axis=0, tiled=True),
        lax.all_gather(w_out, "dp", axis=0, tiled=True),
        lax.all_gather(attn_gain, "dp", axis=0, tiled=True),
    )
    gain_first = gain_first.astype(jnp.float32)
    attn_delta = middle_grad.astype(jnp.bfloat16)
    out_proj_grad = dot_first(attn_delta, attended)
    head_delta = (
        jnp.dot(attn_delta, out_back, preferred_element_type=jnp.float32)
        .astype(jnp.bfloat16)
        .reshape(length, kv_local, group, HEAD_DIM)
    )
    rescored = jnp.where(
        allowed,
        jnp.einsum("qhgd,khd->hgqk", query_group, key_rot, preferred_element_type=jnp.float32)
        * factor,
        masked_score,
    )
    probs = jnp.exp(rescored - log_total)
    prob_grad = jnp.einsum(
        "qhgd,khd->hgqk", head_delta, value_heads, preferred_element_type=jnp.float32
    )
    row_total = jnp.sum(probs * prob_grad, axis=-1, keepdims=True)
    score_delta = (probs * (prob_grad - row_total)).astype(jnp.bfloat16)
    query_rot_grad = (
        jnp.einsum("hgqk,khd->qhgd", score_delta, key_rot, preferred_element_type=jnp.float32)
        * factor
    )
    key_rot_grad = (
        jnp.einsum("hgqk,qhgd->khd", score_delta, query_group, preferred_element_type=jnp.float32)
        * factor
    )
    value_delta = (
        jnp.einsum(
            "hgqk,qhgd->khd",
            probs.astype(jnp.bfloat16),
            head_delta,
            preferred_element_type=jnp.float32,
        )
        .astype(jnp.bfloat16)
        .reshape(length, -1)
    )
    query_delta = (
        rotate(query_rot_grad.reshape(length, -1, HEAD_DIM), cosine, -sine)
        .astype(jnp.bfloat16)
        .reshape(length, -1)
    )
    key_delta = rotate(key_rot_grad, cosine, -sine).astype(jnp.bfloat16).reshape(length, -1)
    query_grad = dot_first(normed_one, query_delta)
    key_grad = dot_first(normed_one, key_delta)
    value_grad = dot_first(normed_one, value_delta)
    local_first = (
        dot_last(query_delta, query_back)
        + dot_last(key_delta, key_back)
        + dot_last(value_delta, value_back)
    )
    normed_one_grad = lax.psum(local_first.astype(jnp.bfloat16), "tensor").astype(jnp.float32)
    input_part, attn_gain_grad = norm_back(normed_one_grad, unit_one, scale_one, gain_first)
    input_grad = middle_grad + input_part
    (
        query_grad,
        key_grad,
        value_grad,
        out_proj_grad,
        gate_grad,
        up_grad,
        down_grad,
        attn_gain_grad,
        mlp_gain_grad,
    ) = (
        lax.psum_scatter(query_grad, "dp", scatter_dimension=0, tiled=True),
        lax.psum_scatter(key_grad, "dp", scatter_dimension=0, tiled=True),
        lax.psum_scatter(value_grad, "dp", scatter_dimension=0, tiled=True),
        lax.psum_scatter(out_proj_grad, "dp", scatter_dimension=0, tiled=True),
        lax.psum_scatter(gate_grad, "dp", scatter_dimension=0, tiled=True),
        lax.psum_scatter(up_grad, "dp", scatter_dimension=0, tiled=True),
        lax.psum_scatter(down_grad, "dp", scatter_dimension=0, tiled=True),
        lax.psum_scatter(attn_gain_grad, "dp", scatter_dimension=0, tiled=True),
        lax.psum_scatter(mlp_gain_grad, "dp", scatter_dimension=0, tiled=True),
    )
    return (
        output,
        input_grad,
        query_grad,
        key_grad,
        value_grad,
        out_proj_grad,
        gate_grad,
        up_grad,
        down_grad,
        attn_gain_grad,
        mlp_gain_grad,
    )


def solution(mesh):
    in_specs = (
        P("dp", None),
        P("dp"),
        P("dp"),
        P("dp", "tensor"),
        P("dp", "tensor"),
        P("dp", "tensor"),
        P("dp", "tensor"),
        P("dp", "tensor"),
        P("dp", "tensor"),
        P("dp", "tensor"),
        P("dp"),
        P("dp"),
        P("dp", None),
    )
    out_specs = (
        P("dp", None),
        P("dp", None),
        P("dp", "tensor"),
        P("dp", "tensor"),
        P("dp", "tensor"),
        P("dp", "tensor"),
        P("dp", "tensor"),
        P("dp", "tensor"),
        P("dp", "tensor"),
        P("dp"),
        P("dp"),
    )
    return jax.shard_map(
        on_device, mesh=mesh, in_specs=in_specs, out_specs=out_specs, check_vma=False
    )
```

profile of v0, /device:TPU:0, one launch (start us, length us, event | category | flops | bytes accessed | tf_op | source)
XLA Modules:
  0.0 2104.6 jit_solution(7362402371754869214)
XLA Ops:
  10.7 23.3 %all-gather = bf16[16,1,128]{2,1,0:T(2,128)(2,1)S(1)} all-gather(bf16[1,1,128]{2,1,0:T(2,128)(2,1)} %bitcast.134), channel_id=1, replica_groups=mesh['dp'=16,'tensor'=2] {'dp'}, dimensions={0}, use_global_device_ids=true | all-gather | bytes 4352 | tf_op jit(solution)/shard_map/all_gather | solution.py:87
  34.0 1.2 fusion.17
  36.2 14.6 all-gather.10.cloned.1.call-done
  50.8 1.7 convolution_convert_fusion.3
  52.6 37.1 %all-gather.12.cloned.1.call-done = bf16[2048,256]{1,0:T(8,128)(2,1)} async-done(((bf16[128,256]{1,0:T(8,128)(2,1)}), bf16[2048,256]{1,0:T(8,128)(2,1)}) %all-gather.12.cloned.1.call-update) | async-done | bytes 1048592 | tf_op jit(solution)/shard_map/all_gather | solution.py:84
  89.8 2.0 fusion.38
  91.8 49.5 %all-gather.14.cloned.1.call-done = bf16[2048,1024]{1,0:T(8,128)(2,1)} async-done(((bf16[128,1024]{1,0:T(8,128)(2,1)}), bf16[2048,1024]{1,0:T(8,128)(2,1)}) %all-gather.14.cloned.1.call-update) | async-done | bytes 4194320 | tf_op jit(solution)/shard_map/all_gather | solution.py:83
  141.3 4.0 fusion.36
  147.0 45.3 %all-gather.16.cloned.1.call-done = bf16[2048,1024]{1,0:T(8,128)(2,1)} async-done(((bf16[128,1024]{1,0:T(8,128)(2,1)}), bf16[2048,1024]{1,0:T(8,128)(2,1)}) %all-gather.16.cloned.1.call-update) | async-done | bytes 4194320 | tf_op jit(solution)/shard_map/all_gather | solution.py:86
  192.3 4.7 fusion.42
  199.1 19.5 all-gather.1
  218.6 17.2 all-reduce.8.cloned.1.call-done
  235.8 1.4 multiply_reduce_fusion.3
  237.4 126.8 %all-gather.20.cloned.1.call-done = bf16[2048,4096]{1,0:T(8,128)(2,1)} async-done(((bf16[128,4096]{1,0:T(8,128)(2,1)}), bf16[2048,4096]{1,0:T(8,128)(2,1)}) %all-gather.20.cloned.1.call-update) | async-done | bytes 16777232 | tf_op jit(solution)/shard_map/all_gather | solution.py:133
  364.3 9.4 fusion.44
  373.7 117.4 %all-gather.18.cloned.1.call-done = bf16[2048,4096]{1,0:T(8,128)(2,1)} async-done(((bf16[128,4096]{1,0:T(8,128)(2,1)}), bf16[2048,4096]{1,0:T(8,128)(2,1)}) %all-gather.18.cloned.1.call-update) | async-done | bytes 16777232 | tf_op jit(solution)/shard_map/all_gather | solution.py:132
  491.1 9.4 fusion.43
  500.5 117.4 %all-gather.22.cloned.1.call-done = bf16[2048,4096]{1,0:T(8,128)(2,1)} async-done(((bf16[128,4096]{1,0:T(8,128)(2,1)}), bf16[2048,4096]{1,0:T(8,128)(2,1)}) %all-gather.22.cloned.1.call-update) | async-done | bytes 16777232 | tf_op jit(solution)/shard_map/all_gather | solution.py:134
  617.9 11.9 multiply_convert_fusion
  629.8 13.2 fusion.45
  643.0 12.9 convolution_add_fusion.1
  656.0 12.5 convolution_convert_fusion
  668.6 25.8 %all-reduce.10.cloned.1.call-done = f32[128,2048]{1,0:T(8,128)} async-done(((f32[128,2048]{1,0:T(8,128)}), f32[128,2048]{1,0:T(8,128)}) %all-reduce.10.cloned.1.call-update) | async-done | bytes 1048592 | tf_op jit(solution)/shard_map/psum | solution.py:161
  694.4 1.7 multiply_reduce_fusion
  696.1 1.7 multiply_add_fusion
  697.8 1.5 convolution_convert_fusion.2
  699.3 1.1 copy.55
  700.5 1.6 fusion.11
  702.1 1.7 multiply_reduce_fusion.1
  706.4 2.4 fusion.1
  709.1 17.1 convolution_bitcast_fusion
  726.3 2.5 fusion.32
  728.8 2.5 fusion.30
  731.4 5.5 fusion.22
  737.5 4.7 fusion.34
  742.3 14.3 fusion.49
  757.0 21.0 fusion.48
  779.9 1.6 fusion.16
  781.5 63.1 %all-reduce.2 = (f32[2048]{0:T(1024)S(1)}, f32[2048]{0:T(1024)S(1)}) all-reduce(f32[2048]{0:T(1024)S(1)} %get-tuple-element.46, f32[2048]{0:T(1024)S(1)} %get-tuple-element.44), channel_id=9, replica_groups=mesh['dp'=16,'tensor'=2] {'dp'}, use_global_device_ids=true, to_apply=%region_19.20.clone | all-reduce | flops 4096 | bytes 32768
  845.8 2.8 fusion.13
  848.6 235.4 %reduce-scatter.20.cloned.1.call-done = f32[128,4096]{0,1:T(8,128)} async-done(((f32[2048,4096]{0,1:T(8,128)}), f32[128,4096]{0,1:T(8,128)}) %reduce-scatter.20.cloned.1.call-update) | async-done | bytes 2097168 | tf_op jit(solution)/shard_map/reduce_scatter | solution.py:245
  1083.9 2.9 copy.59
  1086.8 62.2 %reduce-scatter.10.cloned.1.call-done = f32[128,256]{1,0:T(8,128)} async-done(((f32[2048,256]{1,0:T(8,128)}), f32[128,256]{1,0:T(8,128)}) %reduce-scatter.10.cloned.1.call-update) | async-done | bytes 131088 | tf_op jit(solution)/shard_map/reduce_scatter | solution.py:240
  1149.0 65.0 %reduce-scatter.12.cloned.1.call-done = f32[128,256]{1,0:T(8,128)} async-done(((f32[2048,256]{1,0:T(8,128)}), f32[128,256]{1,0:T(8,128)}) %reduce-scatter.12.cloned.1.call-update) | async-done | bytes 131088 | tf_op jit(solution)/shard_map/reduce_scatter | solution.py:241
  1214.1 106.9 %reduce-scatter.14.cloned.1.call-done = f32[128,1024]{1,0:T(8,128)} async-done(((f32[2048,1024]{1,0:T(8,128)}), f32[128,1024]{1,0:T(8,128)}) %reduce-scatter.14.cloned.1.call-update) | async-done | bytes 524304 | tf_op jit(solution)/shard_map/reduce_scatter | solution.py:242
  1321.0 107.6 %reduce-scatter.8.cloned.1.call-done = f32[128,1024]{1,0:T(8,128)} async-done(((f32[2048,1024]{1,0:T(8,128)}), f32[128,1024]{1,0:T(8,128)}) %reduce-scatter.8.cloned.1.call-update) | async-done | bytes 524304 | tf_op jit(solution)/shard_map/reduce_scatter | solution.py:239
  1428.6 334.9 %reduce-scatter.18.cloned.1.call-done = f32[128,4096]{1,0:T(8,128)} async-done(((f32[2048,4096]{1,0:T(8,128)}), f32[128,4096]{1,0:T(8,128)}) %reduce-scatter.18.cloned.1.call-update) | async-done | bytes 2097168 | tf_op jit(solution)/shard_map/reduce_scatter | solution.py:244
  1763.5 334.3 %reduce-scatter.16.cloned.1.call-done = f32[128,4096]{1,0:T(8,128)} async-done(((f32[2048,4096]{1,0:T(8,128)}), f32[128,4096]{1,0:T(8,128)}) %reduce-scatter.16.cloned.1.call-update) | async-done | bytes 2097168 | tf_op jit(solution)/shard_map/reduce_scatter | solution.py:243
  (109 shorter events, 14.9 us)
Async XLA Ops:
  7.2 134.1 %copy-start = (bf16[128,2048]{1,0:T(8,128)(2,1)S(1)}, bf16[128,2048]{1,0:T(8,128)(2,1)}, u32[]{:S(2)}) copy-start(bf16[128,2048]{1,0:T(8,128)(2,1)} %param.13) | copy-start | bytes 1572868
  7.2 43.6 %all-gather.10.cloned.1.call-start = ((), (), s32[]{:S(2)}) async-start(), calls=%async_computation.7 | async-start | bytes 1114112 | tf_op jit(solution)/shard_map/all_gather | solution.py:85
  7.9 81.8 %all-gather.12.cloned.1.call-start = ((), (), s32[]{:S(2)}) async-start(), calls=%async_computation.8 | async-start | bytes 1114112 | tf_op jit(solution)/shard_map/all_gather | solution.py:84
  8.7 132.6 %all-gather.14.cloned.1.call-start = ((), (), s32[]{:S(2)}) async-start(), calls=%async_computation.9 | async-start | bytes 4456448 | tf_op jit(solution)/shard_map/all_gather | solution.py:83
  9.4 182.9 %all-gather.16.cloned.1.call-start = ((), (), s32[]{:S(2)}) async-start(), calls=%async_computation.10 | async-start | bytes 4456448 | tf_op jit(solution)/shard_map/all_gather | solution.py:86
  10.0 225.8 %all-reduce.8.cloned.1.call-start = ((), (), s32[]{:S(2)}) async-start(), calls=%async_computation.11 | async-start | bytes 2097152 | tf_op jit(solution)/shard_map/psum | solution.py:129
  35.2 110.1 %copy-start.18 = (f32[128]{0:T(128)}, f32[128]{0:T(128)S(1)}, u32[]{:S(2)}) copy-start(f32[128]{0:T(128)S(1)} %add_rsqrt_fusion.1) | copy-start | bytes 1540
  52.6 94.0 %copy-start.13 = (bf16[128,256]{0,1:T(8,128)(2,1)}, bf16[128,256]{0,1:T(8,128)(2,1)S(1)}, u32[]{:S(2)}) copy-start(bf16[128,256]{0,1:T(8,128)(2,1)S(1)} %copy.51) | copy-start | bytes 196612
  91.8 54.9 %copy-start.14 = (bf16[128,4,32]{0,2,1:T(8,128)(2,1)}, bf16[128,4,32]{0,2,1:T(8,128)(2,1)S(1)}, u32[]{:S(2)}) copy-start(bf16[128,4,32]{0,2,1:T(8,128)(2,1)S(1)} %get-tuple-element.63) | copy-start | bytes 98308
  91.8 54.8 %copy-start.16 = (bf16[128,4,32]{0,2,1:T(8,128)(2,1)}, bf16[128,4,32]{0,2,1:T(8,128)(2,1)S(1)}, u32[]{:S(2)}) copy-start(bf16[128,4,32]{0,2,1:T(8,128)(2,1)S(1)} %get-tuple-element.64) | copy-start | bytes 98308
  145.4 0.7 copy-start.9
  145.4 1.0 copy-start.11
  146.4 50.6 %copy-start.2 = (f32[4,4,128,128]{2,3,1,0:T(8,128)}, f32[4,4,128,128]{2,3,1,0:T(8,128)S(1)}, u32[]{:S(2)}) copy-start(f32[4,4,128,128]{2,3,1,0:T(8,128)S(1)} %get-tuple-element.69) | copy-start | bytes 3145732
  147.0 51.4 %copy-start.6 = (bf16[4,64,4,128]{3,1,2,0:T(8,128)(2,1)}, bf16[4,64,4,128]{3,1,2,0:T(8,128)(2,1)S(1)}, u32[]{:S(2)}) copy-start(bf16[4,64,4,128]{3,1,2,0:T(8,128)(2,1)S(1)} %convolution_convert_fusion.1) | copy-start | bytes 786436
  192.3 6.9 copy-start.20
  197.0 167.3 %all-gather.20.cloned.1.call-start = ((), (), s32[]{:S(2)}) async-start(), calls=%async_computation.13 | async-start | bytes 17825792 | tf_op jit(solution)/shard_map/all_gather | solution.py:133
  197.6 293.5 %all-gather.18.cloned.1.call-start = ((), (), s32[]{:S(2)}) async-start(), calls=%async_computation.12 | async-start | bytes 17825792 | tf_op jit(solution)/shard_map/all_gather | solution.py:132
  198.3 419.5 %all-gather.22.cloned.1.call-start = ((), (), s32[]{:S(2)}) async-start(), calls=%async_computation.14 | async-start | bytes 17825792 | tf_op jit(solution)/shard_map/all_gather | solution.py:134
  199.1 495.3 %all-reduce.10.cloned.1.call-start = ((), (), s32[]{:S(2)}) async-start(), calls=%async_computation.15 | async-start | bytes 2097152 | tf_op jit(solution)/shard_map/psum | solution.py:161
  629.8 26.3 %copy-start.5 = (bf16[128,4096]{1,0:T(8,128)(2,1)}, bf16[128,4096]{1,0:T(8,128)(2,1)S(1)}, u32[]{:S(2)}) copy-start(bf16[128,4096]{1,0:T(8,128)(2,1)S(1)} %get-tuple-element.56) | copy-start | bytes 3145732
  655.9 123.9 %all-reduce.12.cloned.1.call-start = ((), (), s32[]{:S(2)}) async-start(), calls=%async_computation.23 | async-start | bytes 2097152 | tf_op jit(solution)/shard_map/psum | solution.py:144
  694.4 3.4 copy-start.4
  700.4 3.4 copy-start.3
  700.4 3.7 copy-start.10
  700.4 3.7 copy-start.12
  700.5 4.0 copy-start.15
  700.5 4.0 copy-start.17
  702.1 2.7 copy-start.7
  703.9 1.5 copy-start.8
  704.1 2.3 copy-start.1
  708.8 375.1 %reduce-scatter.20.cloned.1.call-start = ((), (), s32[]{:S(2)}) async-start(), calls=%async_computation.22 | async-start | bytes 35651584 | tf_op jit(solution)/shard_map/reduce_scatter | solution.py:245
  726.2 422.8 %reduce-scatter.10.cloned.1.call-start = ((), (), s32[]{:S(2)}) async-start(), calls=%async_computation.17 | async-start | bytes 2228224 | tf_op jit(solution)/shard_map/reduce_scatter | solution.py:240
  728.8 485.3 %reduce-scatter.12.cloned.1.call-start = ((), (), s32[]{:S(2)}) async-start(), calls=%async_computation.18 | async-start | bytes 2228224 | tf_op jit(solution)/shard_map/reduce_scatter | solution.py:241
  731.4 589.6 %reduce-scatter.14.cloned.1.call-start = ((), (), s32[]{:S(2)}) async-start(), calls=%async_computation.19 | async-start | bytes 8912896 | tf_op jit(solution)/shard_map/reduce_scatter | solution.py:242
  736.9 0.7 copy-start.19
  736.9 691.7 %reduce-scatter.8.cloned.1.call-start = ((), (), s32[]{:S(2)}) async-start(), calls=%async_computation.16 | async-start | bytes 8912896 | tf_op jit(solution)/shard_map/reduce_scatter | solution.py:239
  742.2 1021.3 %reduce-scatter.18.cloned.1.call-start = ((), (), s32[]{:S(2)}) async-start(), calls=%async_computation.21 | async-start | bytes 35651584 | tf_op jit(solution)/shard_map/reduce_scatter | solution.py:244
  756.7 1341.2 %reduce-scatter.16.cloned.1.call-start = ((), (), s32[]{:S(2)}) async-start(), calls=%async_computation.20 | async-start | bytes 35651584 | tf_op jit(solution)/shard_map/reduce_scatter | solution.py:243
  777.9 0.7 copy-start.21
Sparse Core Ops, SparseCore 0:
  10.2 40.5 all-gather.9
  52.9 36.7 all-gather.11
  91.9 49.3 all-gather.13
  143.3 48.8 all-gather.15
  197.1 38.6 all-reduce.7
  237.8 126.4 all-gather.19
  366.4 124.5 all-gather.17
  493.2 124.5 all-gather.21
  656.1 38.2 all-reduce.9
  708.9 40.0 all-reduce.11
  753.3 330.5 reduce-scatter.19
  1088.1 60.8 reduce-scatter.9
  1153.3 60.6 reduce-scatter.11
  1218.6 102.3 reduce-scatter.13
  1325.5 103.0 reduce-scatter.7
  1433.3 330.1 reduce-scatter.17
  1768.2 329.6 reduce-scatter.15
where the time goes:
time: 2110 us; the launch traced here: 2100 us
  waiting for transfers between devices  1800 us (85%)
  matrix products  159 us (8%)
  blocking collectives  106 us (5%)
    reduce_scatter x1, waiting for transfers between devices, on_device(): lax.psum_scatter(up_grad, 'dp', scatter_dimension=0, tiled=True)  335 us
    reduce_scatter x1, waiting for transfers between devices, on_device(): lax.psum_scatter(gate_grad, 'dp', scatter_dimension=0, tiled=True)  334 us
    reduce_scatter x1, waiting for transfers between devices, on_device(): lax.psum_scatter(down_grad, 'dp', scatter_dimension=0, tiled=True)  235 us
    all_gather x1, waiting for transfers between devices, on_device(): lax.all_gather(w_up, 'dp', axis=0, tiled=True)  127 us
    all_gather x1, waiting for transfers between devices, on_device(): lax.all_gather(w_down, 'dp', axis=0, tiled=True)  117 us
    all_gather x1, waiting for transfers between devices, on_device(): lax.all_gather(w_gate, 'dp', axis=0, tiled=True)  117 us
    reduce_scatter x1, waiting for transfers between devices, on_device(): lax.psum_scatter(query_grad, 'dp', scatter_dimension=0, tiled=True)  108 us
    reduce_scatter x1, waiting for transfers between devices, on_device(): lax.psum_scatter(out_proj_grad, 'dp', scatter_dimension=0, tiled=True)  107 us
  transfers between devices with their start and end apart: 17, of which 16 were waited for; matrix products, arithmetic and copies ran while one was open for 6% of the time, Pallas kernels for 0%

commit v1 on v0

--- a/solution.py
+++ b/solution.py
@@ -10,6 +10,28 @@
 norm_eps = 1e-05
 rope_base = 500000.0
 masked_score = -1e30
+
+
+def joined_along(blocks, dim):
+    blocks = jnp.moveaxis(blocks, 0, dim)
+    shape = blocks.shape
+    return blocks.reshape(*shape[:dim], shape[dim] * shape[dim + 1], *shape[dim + 2 :])
+
+
+def ring_gather(array, axis, dim):
+    size = lax.axis_size(axis)
+    pairs = [(i, (i + 1) % size) for i in range(size)]
+    back = [(b, a) for a, b in pairs]
+    lower, upper = ([], [])
+    for hop in range(size - 1):
+        if hop % 2 == 0:
+            lower.append(lax.ppermute(lower[-1] if lower else array, axis, pairs))
+        else:
+            upper.append(lax.ppermute(upper[-1] if upper else array, axis, back))
+    tiles = jnp.stack([*lower[::-1], array, *upper])
+    shift = lax.axis_index(axis) - len(lower)
+    tiles = tiles[(jnp.arange(size) - shift) % size]
+    return joined_along(tiles, dim)
 
 
 def rope_freqs(head_dim):
@@ -131,7 +153,7 @@
     gate_full, up_full, down_full, gain_two = (
         lax.all_gather(w_gate, "dp", axis=0, tiled=True),
         lax.all_gather(w_up, "dp", axis=0, tiled=True),
-        lax.all_gather(w_down, "dp", axis=0, tiled=True),
+        ring_gather(w_down, "dp", 0),
         lax.all_gather(mlp_gain, "dp", axis=0, tiled=True),
     )
     gain_two = gain_two.astype(jnp.float32)

time: 2110 us -> 2200 us (1.043)
  starting transfers between devices: 1.14 us -> 131 us
  waiting for transfers between devices: 1800 us -> 1690 us
  local copies, waits for them, and re-layouts: 8.4 us -> 53.5 us
    ppermute x0 -> x15, starting transfers between devices: none -> 130 us  [the longest x8 122 us: ring_gather(): lower.append(lax.ppermute(lower[-1] if lower else array, axis, pairs))]
    all_gather x1, waiting for transfers between devices: 117 us -> 0.02 us  [on_device(): lax.all_gather(w_gate, 'dp', axis=0, tiled=True)]
    ppermute x0 -> x15, waiting for transfers between devices: none -> 77.7 us  [the longest x8 77.7 us: ring_gather(): lower.append(lax.ppermute(lower[-1] if lower else array, axis, pairs))]
    all_gather x1, waiting for transfers between devices: 127 us -> 87.2 us  [on_device(): lax.all_gather(w_up, 'dp', axis=0, tiled=True)]
    unnamed x48 -> x73, local copies, waits for them, and re-layouts: 7.18 us -> 36.6 us
  transfers between devices with their start and end apart: 17 -> 32, of which waited for: 16 -> 21; matrix products, arithmetic and copies ran while one was open for 6% -> 9% of each run, Pallas kernels for 0% -> 0%
where the time goes in v1:
time: 2200 us; the launch traced here: 2190 us
  waiting for transfers between devices  1690 us (77%)
  matrix products  168 us (8%)
  starting transfers between devices  131 us (6%)
  blocking collectives  120 us (5%)
  local copies, waits for them, and re-layouts  53.5 us (2%)
    reduce_scatter x1, waiting for transfers between devices, on_device(): lax.psum_scatter(gate_grad, 'dp', scatter_dimension=0, tiled=True)  335 us
    reduce_scatter x1, waiting for transfers between devices, on_device(): lax.psum_scatter(up_grad, 'dp', scatter_dimension=0, tiled=True)  334 us
    reduce_scatter x1, waiting for transfers between devices, on_device(): lax.psum_scatter(down_grad, 'dp', scatter_dimension=0, tiled=True)  235 us
    ppermute x8, starting transfers between devices, ring_gather(): lower.append(lax.ppermute(lower[-1] if lower else array, axis, pairs))  122 us
    all_gather x1, waiting for transfers between devices, on_device(): lax.all_gather(w_down, 'dp', axis=0, tiled=True)  117 us
    reduce_scatter x1, waiting for transfers between devices, on_device(): lax.psum_scatter(out_proj_grad, 'dp', scatter_dimension=0, tiled=True)  108 us
    reduce_scatter x1, waiting for transfers between devices, on_device(): lax.psum_scatter(query_grad, 'dp', scatter_dimension=0, tiled=True)  107 us
    all_gather x1, waiting for transfers between devices, on_device(): lax.all_gather(w_up, 'dp', axis=0, tiled=True)  87.2 us
  transfers between devices with their start and end apart: 32, of which 21 were waited for; matrix products, arithmetic and copies ran while one was open for 9% of the time, Pallas kernels for 0%

profile of v1, /device:TPU:0, one launch (start us, length us, event | category | flops | bytes accessed | tf_op | source)
XLA Modules:
  0.0 2191.5 jit_solution(11989202208589480372)
XLA Ops:
  10.0 23.3 %all-gather = bf16[16,1,128]{2,1,0:T(2,128)(2,1)S(1)} all-gather(bf16[1,1,128]{2,1,0:T(2,128)(2,1)} %bitcast.170), channel_id=1, replica_groups=mesh['dp'=16,'tensor'=2] {'dp'}, dimensions={0}, use_global_device_ids=true | all-gather | bytes 4352 | tf_op jit(solution)/shard_map/all_gather | solution.py:109
  36.2 14.5 all-gather.10.cloned.1.call-done
  52.6 37.1 %all-gather.12.cloned.1.call-done = bf16[2048,256]{1,0:T(8,128)(2,1)} async-done(((bf16[128,256]{1,0:T(8,128)(2,1)}), bf16[2048,256]{1,0:T(8,128)(2,1)}) %all-gather.12.cloned.1.call-update) | async-done | bytes 1048592 | tf_op jit(solution)/shard_map/all_gather | solution.py:106
  91.8 49.5 %all-gather.14.cloned.1.call-done = bf16[2048,1024]{1,0:T(8,128)(2,1)} async-done(((bf16[128,1024]{1,0:T(8,128)(2,1)}), bf16[2048,1024]{1,0:T(8,128)(2,1)}) %all-gather.14.cloned.1.call-update) | async-done | bytes 4194320 | tf_op jit(solution)/shard_map/all_gather | solution.py:105
  141.3 4.1 fusion.38
  147.3 45.0 %all-gather.16.cloned.1.call-done = bf16[2048,1024]{1,0:T(8,128)(2,1)} async-done(((bf16[128,1024]{1,0:T(8,128)(2,1)}), bf16[2048,1024]{1,0:T(8,128)(2,1)}) %all-gather.16.cloned.1.call-update) | async-done | bytes 4194320 | tf_op jit(solution)/shard_map/all_gather | solution.py:108
  192.3 4.7 fusion.44
  199.5 16.7 collective-permute-done
  216.2 4.4 collective-permute-start.8
  220.6 12.6 collective-permute-done.1
  233.2 3.9 collective-permute-start.2
  238.6 11.6 collective-permute-done.2
  250.2 23.6 %collective-permute-start.3 = (bf16[128,4096]{1,0:T(8,128)(2,1)S(1)}, bf16[128,4096]{1,0:T(8,128)(2,1)S(1)}, u32[]{:S(2)}, u32[]{:S(2)}) collective-permute-start(bf16[128,4096]{1,0:T(8,128)(2,1)S(1)} %collective-permute-done.2), channel_id=1, source_target_pairs={{0,2},{2,4},{4,6},{6,8},{8,10},{10,12},{12,14},{14,16},{16,18},{18... | collective-permute-start | bytes 3145736 | tf_op jit(solution)/shard_map/ppermute | solution.py:28
  274.8 14.9 collective-permute-done.3
  289.7 9.3 collective-permute-start.4
  300.8 12.5 collective-permute-done.4
  313.3 31.5 %collective-permute-start.5 = (bf16[128,4096]{1,0:T(8,128)(2,1)S(1)}, bf16[128,4096]{1,0:T(8,128)(2,1)S(1)}, u32[]{:S(2)}, u32[]{:S(2)}) collective-permute-start(bf16[128,4096]{1,0:T(8,128)(2,1)S(1)} %collective-permute-done.4), channel_id=1, source_target_pairs={{0,2},{2,4},{4,6},{6,8},{8,10},{10,12},{12,14},{14,16},{16,18},{18... | collective-permute-start | bytes 3145736 | tf_op jit(solution)/shard_map/ppermute | solution.py:28
  345.8 7.0 collective-permute-done.5
  352.8 37.9 %collective-permute-start.6 = (bf16[128,4096]{1,0:T(8,128)(2,1)S(1)}, bf16[128,4096]{1,0:T(8,128)(2,1)}, u32[]{:S(2)}, u32[]{:S(2)}) collective-permute-start(bf16[128,4096]{1,0:T(8,128)(2,1)S(1)} %collective-permute-done.5), channel_id=1, source_target_pairs={{0,2},{2,4},{4,6},{6,8},{8,10},{10,12},{12,14},{14,16},{16,18},{18... | collective-permute-start | bytes 3145736 | tf_op jit(solution)/shard_map/ppermute | solution.py:28
  393.2 15.8 collective-permute-start.7
  409.0 32.9 %all-gather.1 = bf16[16,1,128]{2,1,0:T(2,128)(2,1)S(1)} all-gather(bf16[1,1,128]{2,1,0:T(2,128)(2,1)S(1)} %bitcast.171), channel_id=1, replica_groups=mesh['dp'=16,'tensor'=2] {'dp'}, dimensions={0}, use_global_device_ids=true | all-gather | bytes 4352 | tf_op jit(solution)/shard_map/all_gather | solution.py:157
  472.0 9.5 fusion.45
  481.4 87.2 %all-gather.20.cloned.1.call-done = bf16[2048,4096]{1,0:T(8,128)(2,1)} async-done(((bf16[128,4096]{1,0:T(8,128)(2,1)}), bf16[2048,4096]{1,0:T(8,128)(2,1)}) %all-gather.20.cloned.1.call-update) | async-done | bytes 16777232 | tf_op jit(solution)/shard_map/all_gather | solution.py:155
  568.7 9.4 fusion.46
  578.1 117.4 %all-gather.22.cloned.1.call-done = bf16[2048,4096]{1,0:T(8,128)(2,1)} async-done(((bf16[128,4096]{1,0:T(8,128)(2,1)}), bf16[2048,4096]{1,0:T(8,128)(2,1)}) %all-gather.22.cloned.1.call-update) | async-done | bytes 16777232 | tf_op jit(solution)/shard_map/all_gather | solution.py:173
  695.5 11.9 multiply_convert_fusion
  707.4 13.2 fusion.47
  720.6 12.9 convolution_add_fusion.1
  735.9 13.4 gather_fusion
  749.3 12.2 convolution_convert_fusion
  761.6 10.4 all-reduce.10.cloned.1.call-done
  775.3 3.6 convolution_convert_fusion.2
  790.5 4.5 fusion.1
  795.3 17.1 convolution_bitcast_fusion
  817.7 5.3 fusion.36
  823.1 5.5 fusion.22
  828.7 14.4 fusion.50
  843.4 21.0 fusion.51
  867.9 63.7 %all-reduce.2 = (f32[2048]{0:T(1024)S(1)}, f32[2048]{0:T(1024)S(1)}) all-reduce(f32[2048]{0:T(1024)S(1)} %get-tuple-element.46, f32[2048]{0:T(1024)S(1)} %get-tuple-element.44), channel_id=9, replica_groups=mesh['dp'=16,'tensor'=2] {'dp'}, use_global_device_ids=true, to_apply=%region_19.20.clone | all-reduce | flops 4096 | bytes 32768
  932.7 2.8 fusion.13
  935.5 235.4 %reduce-scatter.20.cloned.1.call-done = f32[128,4096]{0,1:T(8,128)} async-done(((f32[2048,4096]{0,1:T(8,128)}), f32[128,4096]{0,1:T(8,128)}) %reduce-scatter.20.cloned.1.call-update) | async-done | bytes 2097168 | tf_op jit(solution)/shard_map/reduce_scatter | solution.py:267
  1170.9 2.9 copy.59
  1173.7 62.1 %reduce-scatter.10.cloned.1.call-done = f32[128,256]{1,0:T(8,128)} async-done(((f32[2048,256]{1,0:T(8,128)}), f32[128,256]{1,0:T(8,128)}) %reduce-scatter.10.cloned.1.call-update) | async-done | bytes 131088 | tf_op jit(solution)/shard_map/reduce_scatter | solution.py:262
  1235.9 65.0 %reduce-scatter.12.cloned.1.call-done = f32[128,256]{1,0:T(8,128)} async-done(((f32[2048,256]{1,0:T(8,128)}), f32[128,256]{1,0:T(8,128)}) %reduce-scatter.12.cloned.1.call-update) | async-done | bytes 131088 | tf_op jit(solution)/shard_map/reduce_scatter | solution.py:263
  1300.9 107.0 %reduce-scatter.8.cloned.1.call-done = f32[128,1024]{1,0:T(8,128)} async-done(((f32[2048,1024]{1,0:T(8,128)}), f32[128,1024]{1,0:T(8,128)}) %reduce-scatter.8.cloned.1.call-update) | async-done | bytes 524304 | tf_op jit(solution)/shard_map/reduce_scatter | solution.py:261
  1407.9 107.6 %reduce-scatter.14.cloned.1.call-done = f32[128,1024]{1,0:T(8,128)} async-done(((f32[2048,1024]{1,0:T(8,128)}), f32[128,1024]{1,0:T(8,128)}) %reduce-scatter.14.cloned.1.call-update) | async-done | bytes 524304 | tf_op jit(solution)/shard_map/reduce_scatter | solution.py:264
  1515.5 334.9 %reduce-scatter.16.cloned.1.call-done = f32[128,4096]{1,0:T(8,128)} async-done(((f32[2048,4096]{1,0:T(8,128)}), f32[128,4096]{1,0:T(8,128)}) %reduce-scatter.16.cloned.1.call-update) | async-done | bytes 2097168 | tf_op jit(solution)/shard_map/reduce_scatter | solution.py:265
  1850.4 334.3 %reduce-scatter.18.cloned.1.call-done = f32[128,4096]{1,0:T(8,128)} async-done(((f32[2048,4096]{1,0:T(8,128)}), f32[128,4096]{1,0:T(8,128)}) %reduce-scatter.18.cloned.1.call-update) | async-done | bytes 2097168 | tf_op jit(solution)/shard_map/reduce_scatter | solution.py:266
  (168 shorter events, 78.2 us)
Async XLA Ops:
  7.2 192.0 %copy-start.3 = (bf16[128,4096]{1,0:T(8,128)(2,1)S(1)}, bf16[128,4096]{1,0:T(8,128)(2,1)}, u32[]{:S(2)}) copy-start(bf16[128,4096]{1,0:T(8,128)(2,1)} %param.22) | copy-start | bytes 3145732
  7.2 401.9 %copy-start.25 = (bf16[128]{0:T(256)(128)(2,1)S(1)}, bf16[128]{0:T(256)(128)(2,1)}, u32[]{:S(2)}) copy-start(bf16[128]{0:T(256)(128)(2,1)} %param.24) | copy-start | bytes 772
  7.2 43.6 %all-gather.10.cloned.1.call-start = ((), (), s32[]{:S(2)}) async-start(), calls=%async_computation.7 | async-start | bytes 1114112 | tf_op jit(solution)/shard_map/all_gather | solution.py:107
  7.9 81.8 %all-gather.12.cloned.1.call-start = ((), (), s32[]{:S(2)}) async-start(), calls=%async_computation.8 | async-start | bytes 1114112 | tf_op jit(solution)/shard_map/all_gather | solution.py:106
  8.7 132.7 %all-gather.14.cloned.1.call-start = ((), (), s32[]{:S(2)}) async-start(), calls=%async_computation.9 | async-start | bytes 4456448 | tf_op jit(solution)/shard_map/all_gather | solution.py:105
  9.4 182.9 %all-gather.16.cloned.1.call-start = ((), (), s32[]{:S(2)}) async-start(), calls=%async_computation.10 | async-start | bytes 4456448 | tf_op jit(solution)/shard_map/all_gather | solution.py:108
  10.0 460.3 %all-reduce.8.cloned.1.call-start = ((), (), s32[]{:S(2)}) async-start(), calls=%async_computation.11 | async-start | bytes 2097152 | tf_op jit(solution)/shard_map/psum | solution.py:151
  35.3 110.2 %copy-start.23 = (f32[128]{0:T(128)}, f32[128]{0:T(128)S(1)}, u32[]{:S(2)}) copy-start(f32[128]{0:T(128)S(1)} %add_rsqrt_fusion.1) | copy-start | bytes 1540
  52.6 146.5 %copy-start.20 = (bf16[128,256]{0,1:T(8,128)(2,1)}, bf16[128,256]{0,1:T(8,128)(2,1)S(1)}, u32[]{:S(2)}) copy-start(bf16[128,256]{0,1:T(8,128)(2,1)S(1)} %copy.51) | copy-start | bytes 196612
  91.8 107.3 %copy-start.21 = (bf16[128,4,32]{0,2,1:T(8,128)(2,1)}, bf16[128,4,32]{0,2,1:T(8,128)(2,1)S(1)}, u32[]{:S(2)}) copy-start(bf16[128,4,32]{0,2,1:T(8,128)(2,1)S(1)} %get-tuple-element.63) | copy-start | bytes 98308
  91.8 107.3 %copy-start.22 = (bf16[128,4,32]{0,2,1:T(8,128)(2,1)}, bf16[128,4,32]{0,2,1:T(8,128)(2,1)S(1)}, u32[]{:S(2)}) copy-start(bf16[128,4,32]{0,2,1:T(8,128)(2,1)S(1)} %get-tuple-element.64) | copy-start | bytes 98308
  145.6 315.8 %copy-start.18 = (bf16[128,16,32]{0,2,1:T(8,128)(2,1)}, bf16[128,16,32]{0,2,1:T(8,128)(2,1)S(1)}, u32[]{:S(2)}) copy-start(bf16[128,16,32]{0,2,1:T(8,128)(2,1)S(1)} %get-tuple-element.59) | copy-start | bytes 393220
  145.6 315.8 %copy-start.19 = (bf16[128,16,32]{0,2,1:T(8,128)(2,1)}, bf16[128,16,32]{0,2,1:T(8,128)(2,1)S(1)}, u32[]{:S(2)}) copy-start(bf16[128,16,32]{0,2,1:T(8,128)(2,1)S(1)} %get-tuple-element.60) | copy-start | bytes 393220
  147.3 49.8 %copy-start.4 = (bf16[4,64,4,128]{3,1,2,0:T(8,128)(2,1)}, bf16[4,64,4,128]{3,1,2,0:T(8,128)(2,1)S(1)}, u32[]{:S(2)}) copy-start(bf16[4,64,4,128]{3,1,2,0:T(8,128)(2,1)S(1)} %convolution_convert_fusion.1) | copy-start | bytes 786436
  197.0 275.0 %all-gather.18.cloned.1.call-start = ((), (), s32[]{:S(2)}) async-start(), calls=%async_computation.12 | async-start | bytes 17825792 | tf_op jit(solution)/shard_map/all_gather | solution.py:154
  197.6 272.7 %copy-start = (bf16[128,2048]{1,0:T(8,128)(2,1)S(1)}, bf16[128,2048]{1,0:T(8,128)(2,1)}, u32[]{:S(2)}) copy-start(bf16[128,2048]{1,0:T(8,128)(2,1)} %param.13) | copy-start | bytes 1572868
  197.6 371.1 %all-gather.20.cloned.1.call-start = ((), (), s32[]{:S(2)}) async-start(), calls=%async_computation.13 | async-start | bytes 17825792 | tf_op jit(solution)/shard_map/all_gather | solution.py:155
  198.3 497.1 %all-gather.22.cloned.1.call-start = ((), (), s32[]{:S(2)}) async-start(), calls=%async_computation.14 | async-start | bytes 17825792 | tf_op jit(solution)/shard_map/all_gather | solution.py:173
  199.1 572.9 %all-reduce.10.cloned.1.call-start = ((), (), s32[]{:S(2)}) async-start(), calls=%async_computation.15 | async-start | bytes 2097152 | tf_op jit(solution)/shard_map/psum | solution.py:183
  199.2 17.0 collective-permute-start
  216.1 17.0 collective-permute-start.1
  216.2 21.0 collective-permute-start.8
  233.2 40.6 %copy-start.7 = (bf16[128,4096]{1,0:T(8,128)(2,1)}, bf16[128,4096]{1,0:T(8,128)(2,1)S(1)}, u32[]{:S(2)}) copy-start(bf16[128,4096]{1,0:T(8,128)(2,1)S(1)} %collective-permute-done.1) | copy-start | bytes 3145732
  233.2 17.0 collective-permute-start.2
  238.1 35.7 %collective-permute-start.9 = (bf16[128,4096]{1,0:T(8,128)(2,1)S(1)}, bf16[128,4096]{1,0:T(8,128)(2,1)S(1)}, u32[]{:S(2)}, u32[]{:S(2)}) collective-permute-start(bf16[128,4096]{1,0:T(8,128)(2,1)S(1)} %collective-permute-done.8), channel_id=1, source_target_pairs={{2,0},{4,2},{6,4},{8,6},{10,8},{12,10},{14,12},{16,14},{18,16},{20... | collective-permute-start | bytes 3145736 | tf_op jit(solution)/shard_map/ppermute | solution.py:30
  250.2 48.9 %copy-start.10 = (bf16[128,4096]{1,0:T(8,128)(2,1)}, bf16[128,4096]{1,0:T(8,128)(2,1)S(1)}, u32[]{:S(2)}) copy-start(bf16[128,4096]{1,0:T(8,128)(2,1)S(1)} %collective-permute-done.2) | copy-start | bytes 3145732
  250.2 39.5 %collective-permute-start.3 = (bf16[128,4096]{1,0:T(8,128)(2,1)S(1)}, bf16[128,4096]{1,0:T(8,128)(2,1)S(1)}, u32[]{:S(2)}, u32[]{:S(2)}) collective-permute-start(bf16[128,4096]{1,0:T(8,128)(2,1)S(1)} %collective-permute-done.2), channel_id=1, source_target_pairs={{0,2},{2,4},{4,6},{6,8},{8,10},{10,12},{12,14},{14,16},{16,18},{18... | collective-permute-start | bytes 3145736 | tf_op jit(solution)/shard_map/ppermute | solution.py:28
  273.8 25.2 %collective-permute-start.10 = (bf16[128,4096]{1,0:T(8,128)(2,1)S(1)}, bf16[128,4096]{1,0:T(8,128)(2,1)S(1)}, u32[]{:S(2)}, u32[]{:S(2)}) collective-permute-start(bf16[128,4096]{1,0:T(8,128)(2,1)S(1)} %collective-permute-done.9), channel_id=1, source_target_pairs={{2,0},{4,2},{6,4},{8,6},{10,8},{12,10},{14,12},{16,14},{18,16},{20... | collective-permute-start | bytes 3145736 | tf_op jit(solution)/shard_map/ppermute | solution.py:30
  289.7 101.1 %copy-start.15 = (bf16[128,4096]{1,0:T(8,128)(2,1)}, bf16[128,4096]{1,0:T(8,128)(2,1)S(1)}, u32[]{:S(2)}) copy-start(bf16[128,4096]{1,0:T(8,128)(2,1)S(1)} %collective-permute-done.3) | copy-start | bytes 3145732
  289.7 23.6 %collective-permute-start.4 = (bf16[128,4096]{1,0:T(8,128)(2,1)S(1)}, bf16[128,4096]{1,0:T(8,128)(2,1)S(1)}, u32[]{:S(2)}, u32[]{:S(2)}) collective-permute-start(bf16[128,4096]{1,0:T(8,128)(2,1)S(1)} %collective-permute-done.3), channel_id=1, source_target_pairs={{0,2},{2,4},{4,6},{6,8},{8,10},{10,12},{12,14},{14,16},{16,18},{18... | collective-permute-start | bytes 3145736 | tf_op jit(solution)/shard_map/ppermute | solution.py:28
  299.1 45.7 %collective-permute-start.11 = (bf16[128,4096]{1,0:T(8,128)(2,1)S(1)}, bf16[128,4096]{1,0:T(8,128)(2,1)S(1)}, u32[]{:S(2)}, u32[]{:S(2)}) collective-permute-start(bf16[128,4096]{1,0:T(8,128)(2,1)S(1)} %collective-permute-done.10), channel_id=1, source_target_pairs={{2,0},{4,2},{6,4},{8,6},{10,8},{12,10},{14,12},{16,14},{18,16},{20... | collective-permute-start | bytes 3145736 | tf_op jit(solution)/shard_map/ppermute | solution.py:30
  313.3 77.5 %copy-start.16 = (bf16[128,4096]{1,0:T(8,128)(2,1)}, bf16[128,4096]{1,0:T(8,128)(2,1)S(1)}, u32[]{:S(2)}) copy-start(bf16[128,4096]{1,0:T(8,128)(2,1)S(1)} %collective-permute-done.4) | copy-start | bytes 3145732
  313.3 39.5 %collective-permute-start.5 = (bf16[128,4096]{1,0:T(8,128)(2,1)S(1)}, bf16[128,4096]{1,0:T(8,128)(2,1)S(1)}, u32[]{:S(2)}, u32[]{:S(2)}) collective-permute-start(bf16[128,4096]{1,0:T(8,128)(2,1)S(1)} %collective-permute-done.4), channel_id=1, source_target_pairs={{0,2},{2,4},{4,6},{6,8},{8,10},{10,12},{12,14},{14,16},{16,18},{18... | collective-permute-start | bytes 3145736 | tf_op jit(solution)/shard_map/ppermute | solution.py:28
  345.8 45.0 %collective-permute-start.12 = (bf16[128,4096]{1,0:T(8,128)(2,1)S(1)}, bf16[128,4096]{1,0:T(8,128)(2,1)}, u32[]{:S(2)}, u32[]{:S(2)}) collective-permute-start(bf16[128,4096]{1,0:T(8,128)(2,1)S(1)} %collective-permute-done.11), channel_id=1, source_target_pairs={{2,0},{4,2},{6,4},{8,6},{10,8},{12,10},{14,12},{16,14},{18,16},{20... | collective-permute-start | bytes 3145736 | tf_op jit(solution)/shard_map/ppermute | solution.py:30
  352.8 40.4 %copy-start.17 = (bf16[128,4096]{1,0:T(8,128)(2,1)}, bf16[128,4096]{1,0:T(8,128)(2,1)S(1)}, u32[]{:S(2)}) copy-start(bf16[128,4096]{1,0:T(8,128)(2,1)S(1)} %collective-permute-done.5) | copy-start | bytes 3145732
  352.8 40.4 %collective-permute-start.6 = (bf16[128,4096]{1,0:T(8,128)(2,1)S(1)}, bf16[128,4096]{1,0:T(8,128)(2,1)}, u32[]{:S(2)}, u32[]{:S(2)}) collective-permute-start(bf16[128,4096]{1,0:T(8,128)(2,1)S(1)} %collective-permute-done.5), channel_id=1, source_target_pairs={{0,2},{2,4},{4,6},{6,8},{8,10},{10,12},{12,14},{14,16},{16,18},{18... | collective-permute-start | bytes 3145736 | tf_op jit(solution)/shard_map/ppermute | solution.py:28
  390.8 51.3 %collective-permute-start.13 = (bf16[128,4096]{1,0:T(8,128)(2,1)}, bf16[128,4096]{1,0:T(8,128)(2,1)}, u32[]{:S(2)}, u32[]{:S(2)}) collective-permute-start(bf16[128,4096]{1,0:T(8,128)(2,1)} %collective-permute-done.12), channel_id=1, source_target_pairs={{2,0},{4,2},{6,4},{8,6},{10,8},{12,10},{14,12},{16,14},{18,16},{20... | collective-permute-start | bytes 3145736 | tf_op jit(solution)/shard_map/ppermute | solution.py:30
  393.2 49.6 %collective-permute-start.7 = (bf16[128,4096]{1,0:T(8,128)(2,1)}, bf16[128,4096]{1,0:T(8,128)(2,1)}, u32[]{:S(2)}, u32[]{:S(2)}) collective-permute-start(bf16[128,4096]{1,0:T(8,128)(2,1)} %collective-permute-done.6), channel_id=1, source_target_pairs={{0,2},{2,4},{4,6},{6,8},{8,10},{10,12},{12,14},{14,16},{16,18},{18... | collective-permute-start | bytes 3145736 | tf_op jit(solution)/shard_map/ppermute | solution.py:28
  442.1 291.5 %collective-permute-start.14 = (bf16[128,4096]{1,0:T(8,128)(2,1)}, bf16[128,4096]{1,0:T(8,128)(2,1)}, u32[]{:S(2)}, u32[]{:S(2)}) collective-permute-start(bf16[128,4096]{1,0:T(8,128)(2,1)} %collective-permute-done.13), channel_id=1, source_target_pairs={{2,0},{4,2},{6,4},{8,6},{10,8},{12,10},{14,12},{16,14},{18,16},{20... | collective-permute-start | bytes 3145736 | tf_op jit(solution)/shard_map/ppermute | solution.py:30
  707.4 42.0 %copy-start.2 = (bf16[128,4096]{1,0:T(8,128)(2,1)}, bf16[128,4096]{1,0:T(8,128)(2,1)S(1)}, u32[]{:S(2)}) copy-start(bf16[128,4096]{1,0:T(8,128)(2,1)S(1)} %get-tuple-element.56) | copy-start | bytes 3145732
  733.6 132.8 %all-reduce.12.cloned.1.call-start = ((), (), s32[]{:S(2)}) async-start(), calls=%async_computation.23 | async-start | bytes 2097152 | tf_op jit(solution)/shard_map/psum | solution.py:166
  795.1 375.8 %reduce-scatter.20.cloned.1.call-start = ((), (), s32[]{:S(2)}) async-start(), calls=%async_computation.22 | async-start | bytes 35651584 | tf_op jit(solution)/shard_map/reduce_scatter | solution.py:267
  812.5 423.4 %reduce-scatter.10.cloned.1.call-start = ((), (), s32[]{:S(2)}) async-start(), calls=%async_computation.17 | async-start | bytes 2228224 | tf_op jit(solution)/shard_map/reduce_scatter | solution.py:262
  815.1 485.8 %reduce-scatter.12.cloned.1.call-start = ((), (), s32[]{:S(2)}) async-start(), calls=%async_computation.18 | async-start | bytes 2228224 | tf_op jit(solution)/shard_map/reduce_scatter | solution.py:263
  817.7 590.2 %reduce-scatter.8.cloned.1.call-start = ((), (), s32[]{:S(2)}) async-start(), calls=%async_computation.16 | async-start | bytes 8912896 | tf_op jit(solution)/shard_map/reduce_scatter | solution.py:261
  823.1 692.4 %reduce-scatter.14.cloned.1.call-start = ((), (), s32[]{:S(2)}) async-start(), calls=%async_computation.19 | async-start | bytes 8912896 | tf_op jit(solution)/shard_map/reduce_scatter | solution.py:264
  828.6 1021.7 %reduce-scatter.16.cloned.1.call-start = ((), (), s32[]{:S(2)}) async-start(), calls=%async_computation.20 | async-start | bytes 35651584 | tf_op jit(solution)/shard_map/reduce_scatter | solution.py:265
  843.1 1341.6 %reduce-scatter.18.cloned.1.call-start = ((), (), s32[]{:S(2)}) async-start(), calls=%async_computation.21 | async-start | bytes 35651584 | tf_op jit(solution)/shard_map/reduce_scatter | solution.py:266
  (11 other events, 92.2 us)
Sparse Core Ops, SparseCore 0:
  10.2 40.5 all-gather.9
  52.9 36.8 all-gather.11
  91.9 49.3 all-gather.13
  143.3 48.8 all-gather.15
  197.1 38.6 all-reduce.7
  237.8 192.3 all-gather.17
  432.4 136.2 all-gather.19
  570.8 124.5 all-gather.21
  733.7 38.2 all-reduce.9
  795.2 40.0 all-reduce.11
  839.6 331.2 reduce-scatter.19
  1175.0 60.8 reduce-scatter.9
  1240.2 60.6 reduce-scatter.11
  1305.4 102.4 reduce-scatter.7
  1412.4 103.0 reduce-scatter.13
  1520.2 330.1 reduce-scatter.15
  1855.0 329.5 reduce-scatter.17
